TPU v7x, 32 devices: a whole 2x2x4 slice. The times are simulated.
32 devices in a mesh: dp: 4 (over x, core), expert: 8 (over z, y).
Axes of the slice: x: 2, y: 2, z: 4, core: 2. Of those that a mesh axis runs over, the one named last changes fastest.
Arguments:
- tokens: bfloat16 [16384, 768], P(('dp', 'expert')), may hold values from -6 to 6
- cotangent: bfloat16 [16384, 768], P(('dp', 'expert')), may hold values from -6 to 6
- chosen: int32 [16384, 2], P(('dp', 'expert')), may hold values from 0 to 9, all different within a row; in each aligned block of 512 rows (0 to 511, 512 to 1023, ...) at most 128 rows name the same one
- gates: float32 [16384, 2], P(('dp', 'expert')), may hold values from 0.2 to 0.8
- lengths: int32 [32, 8], P(('dp', 'expert')), may hold values from 1 to 256, 512 in all within a row
- keep_mask: int32 [16384], P(('dp', 'expert')), may hold values 0 or 1
- gain1: float32 [768], replicated, may hold values from 0.5 to 1.5
- w_qkv: bfloat16 [768, 2304], replicated, may hold values from -0.21875 to 0.21875
- w_o: bfloat16 [768, 768], replicated, may hold values from -0.875 to 0.875
- gain2: float32 [768], replicated, may hold values from 0.5 to 1.5
- frozen_in: bfloat16 [2, 3072, 768], replicated, may hold values from -0.21875 to 0.21875
- frozen_out: bfloat16 [2, 3072, 768], replicated, may hold values from -0.109375 to 0.109375
- w_in: bfloat16 [8, 3072, 768], P('expert', 'dp'), may hold values from -0.21875 to 0.21875
- w_out: bfloat16 [8, 3072, 768], P('expert', 'dp'), may hold values from -0.109375 to 0.109375
Outputs:
- output: bfloat16 [16384, 768], P(('dp', 'expert'))
- d_tokens: bfloat16 [16384, 768], P(('dp', 'expert'))
- d_gain1: float32 [768], replicated
- d_w_qkv: float32 [768, 2304], replicated
- d_w_o: float32 [768, 768], replicated
- d_gain2: float32 [768], replicated
- d_w_in: float32 [8, 3072, 768], P('expert', 'dp')
- d_w_out: float32 [8, 3072, 768], P('expert', 'dp')
- counts: float32 [10], replicated
Inputs may be any that keep to these rules, and one draw needn't show every extreme that they name: `chosen`: each token names two different experts; among the 512 tokens of one device no expert is named more than 128 times, a bound that some block reaches. The 8 lengths of a device sum to 512; the longest is exactly 256.
All inputs are finite; a program needn't handle non-finite values. No bound on the sum of `keep_mask` on one device may be relied on, other than what follows from the above.
Results may differ from a plain program's by a relative error of at most 0.012.
Values may be sent and summed in bfloat16 or wider, within the bound.
A program may use at most 256 MiB of HBM per device.

v0:
```python
import jax
import jax.numpy as jnp
from jax import lax
from jax.sharding import PartitionSpec as P

HEADS = 12
HEAD_DIM = 64
FROZEN = 2


def layer_norm(values_in, gain_vec):
    row_mean = jnp.mean(values_in, axis=-1, keepdims=True)
    centred = values_in - row_mean
    variance = jnp.mean(centred * centred, axis=-1, keepdims=True)
    return centred * lax.rsqrt(variance + 1e-05) * gain_vec


def expert_forward(rows_low, up_weights, down_weights):
    hidden = jnp.einsum("gcd,gfd->gcf", rows_low, up_weights, preferred_element_type=jnp.float32)
    active = jax.nn.gelu(hidden).astype(jnp.bfloat16)
    result_rows = jnp.einsum(
        "gcf,gfd->gcd", active, down_weights, preferred_element_type=jnp.float32
    ).astype(jnp.bfloat16)
    return (result_rows, hidden)


def expert_backward(result_grad, hidden, up_weights, down_weights):
    active_grad = jnp.einsum(
        "gcd,gfd->gcf", result_grad, down_weights, preferred_element_type=jnp.float32
    )
    active, gelu_back = jax.vjp(jax.nn.gelu, hidden)
    hidden_grad = gelu_back(active_grad)[0].astype(jnp.bfloat16)
    input_grad = jnp.einsum(
        "gcf,gfd->gcd", hidden_grad, up_weights, preferred_element_type=jnp.float32
    ).astype(jnp.bfloat16)
    return (input_grad, hidden_grad, active.astype(jnp.bfloat16))


def block_scores(query_part, key_heads, allowed):
    scores = (
        jnp.einsum("qhd,khd->hqk", query_part, key_heads, preferred_element_type=jnp.float32)
        * 0.125
    )
    return jnp.where(allowed[None], scores, -1e30)


def body(
    tokens,
    cotangent,
    chosen,
    gates,
    lengths,
    keep_mask,
    gain1,
    w_qkv,
    w_o,
    gain2,
    frozen_in,
    frozen_out,
    w_in,
    w_out,
):
    row_count = tokens.shape[0]
    feat_width = tokens.shape[1]
    owners = lax.axis_size("expert")
    kind_count = FROZEN + owners
    slot_count = (2 * row_count * 5 // (4 * kind_count) + 7) // 8 * 8
    block_rows = min(512, row_count)
    weights_in, weights_out = (
        lax.all_gather(w_in, "dp", axis=1, tiled=True),
        lax.all_gather(w_out, "dp", axis=1, tiled=True),
    )
    tokens_full = tokens.astype(jnp.float32)
    normed_one, norm_one_back = jax.vjp(layer_norm, tokens_full, gain1)
    normed_one_low = normed_one.astype(jnp.bfloat16)
    projected = jnp.dot(normed_one_low, w_qkv, preferred_element_type=jnp.float32).astype(
        jnp.bfloat16
    )
    queries = projected[:, :feat_width].reshape(row_count, HEADS, HEAD_DIM)
    key_heads = projected[:, feat_width : 2 * feat_width].reshape(row_count, HEADS, HEAD_DIM)
    value_heads = projected[:, 2 * feat_width :].reshape(row_count, HEADS, HEAD_DIM)
    places = jnp.arange(row_count, dtype=jnp.int32)
    doc_ends = jnp.cumsum(lengths[0])
    documents = jnp.sum((places[:, None] >= doc_ends[None, :]).astype(jnp.int32), axis=1)

    def permitted():
        return (
            (documents[:, None] == documents[None, :])
            & (places[None, :] <= places[:, None])
            & ((keep_mask[None, :] > 0) | (places[None, :] == places[:, None]))
        )

    scores = block_scores(queries, key_heads, permitted())
    peak_score = jnp.max(scores, axis=-1, keepdims=True)
    exp_scores = jnp.exp(scores - peak_score)
    exp_total = jnp.sum(exp_scores, axis=-1, keepdims=True)
    probs_low = (exp_scores / exp_total).astype(jnp.bfloat16)
    block_out = jnp.einsum(
        "hqk,khd->qhd", probs_low, value_heads, preferred_element_type=jnp.float32
    )
    out_blocks = block_out.reshape(block_rows, feat_width).astype(jnp.bfloat16)
    lse_blocks = [peak_score + jnp.log(exp_total)]
    mixed_rows = tokens_full + jnp.dot(out_blocks, w_o, preferred_element_type=jnp.float32)
    normed_two, norm_two_back = jax.vjp(layer_norm, mixed_rows, gain2)
    normed_two_low = normed_two.astype(jnp.bfloat16)
    flat_ids = chosen.reshape(-1)
    one_hot = (flat_ids[:, None] == jnp.arange(kind_count, dtype=jnp.int32)[None, :]).astype(
        jnp.int32
    )
    slot_ranks = jnp.sum(jnp.cumsum(one_hot, axis=0) * one_hot, axis=1) - 1
    positions = flat_ids * slot_count + slot_ranks
    buffer_rows = (
        jnp.zeros((kind_count * slot_count, feat_width), jnp.bfloat16)
        .at[positions]
        .set(jnp.repeat(normed_two_low, 2, axis=0))
    )
    local_rows = buffer_rows[: FROZEN * slot_count].reshape(FROZEN, slot_count, feat_width)
    routed_rows = buffer_rows[FROZEN * slot_count :].reshape(owners, slot_count, feat_width)
    arrived_rows = lax.all_to_all(routed_rows, "expert", split_axis=0, concat_axis=0, tiled=True)
    result_rows, _ = expert_forward(
        arrived_rows.reshape(1, -1, feat_width), weights_in, weights_out
    )
    served = result_rows.reshape(arrived_rows.shape)
    frozen_result, frozen_hidden = expert_forward(local_rows, frozen_in, frozen_out)
    returned = lax.all_to_all(served, "expert", split_axis=0, concat_axis=0, tiled=True)
    results = jnp.concatenate(
        [frozen_result.reshape(-1, feat_width), returned.reshape(-1, feat_width)], axis=0
    )
    picked = results[positions].astype(jnp.float32).reshape(row_count, 2, feat_width)
    output = mixed_rows + jnp.sum(picked * gates[:, :, None], axis=1)
    grad_out = cotangent.astype(jnp.float32)
    weighted = (jnp.repeat(grad_out, 2, axis=0) * gates.reshape(-1, 1)).astype(jnp.bfloat16)
    grad_buffer = (
        jnp.zeros((kind_count * slot_count, feat_width), jnp.bfloat16).at[positions].set(weighted)
    )
    frozen_grad_rows = grad_buffer[: FROZEN * slot_count].reshape(FROZEN, slot_count, feat_width)
    routed_grad = grad_buffer[FROZEN * slot_count :].reshape(owners, slot_count, feat_width)
    arrived_grad = lax.all_to_all(routed_grad, "expert", split_axis=0, concat_axis=0, tiled=True)
    flat_rows = arrived_rows.reshape(1, -1, feat_width)
    flat_grad = arrived_grad.reshape(1, -1, feat_width)
    hidden_all = jnp.einsum(
        "gcd,gfd->gcf", flat_rows, weights_in, preferred_element_type=jnp.float32
    )
    row_input_grad, hidden_grad, active = expert_backward(
        flat_grad, hidden_all, weights_in, weights_out
    )
    sent_back = lax.all_to_all(
        row_input_grad.reshape(owners, slot_count, feat_width),
        "expert",
        split_axis=0,
        concat_axis=0,
        tiled=True,
    )
    frozen_input_grad, _, _ = expert_backward(
        frozen_grad_rows, frozen_hidden, frozen_in, frozen_out
    )
    hidden_rows = hidden_grad[0]
    active_rows = active[0]
    input_rows = flat_rows[0]
    output_rows = flat_grad[0]
    term_in = lax.dot_general(
        hidden_rows, input_rows, (((0,), (0,)), ((), ())), preferred_element_type=jnp.float32
    )
    term_out = lax.dot_general(
        active_rows, output_rows, (((0,), (0,)), ((), ())), preferred_element_type=jnp.float32
    )
    summed = lax.psum_scatter(
        jnp.concatenate([term_in, term_out], axis=1), "dp", scatter_dimension=0, tiled=True
    )
    d_w_in = summed[:, :feat_width][None]
    d_w_out = summed[:, feat_width:][None]
    row_grads = jnp.concatenate(
        [frozen_input_grad.reshape(-1, feat_width), sent_back.reshape(-1, feat_width)], axis=0
    )
    normed_two_grad = jnp.sum(
        row_grads[positions].astype(jnp.float32).reshape(row_count, 2, feat_width), axis=1
    )
    mixed_part, gain2_grad = norm_two_back(normed_two_grad)
    mixed_grad = grad_out + mixed_part
    branch_grad = mixed_grad.astype(jnp.bfloat16)
    w_o_grad = lax.dot_general(
        out_blocks, branch_grad, (((0,), (0,)), ((), ())), preferred_element_type=jnp.float32
    )
    attended_grad = lax.dot_general(
        branch_grad, w_o, (((1,), (1,)), ((), ())), preferred_element_type=jnp.float32
    ).astype(jnp.bfloat16)
    attended_heads = attended_grad.reshape(row_count, HEADS, HEAD_DIM)
    key_grad = jnp.zeros((row_count, HEADS, HEAD_DIM), jnp.float32)
    value_grad = jnp.zeros((row_count, HEADS, HEAD_DIM), jnp.float32)
    query_grads = []
    for block_index, row_start in enumerate(range(0, row_count, block_rows)):
        scores = block_scores(queries, key_heads, permitted())
        probs_full = jnp.exp(scores - lse_blocks[block_index])
        probs_low = probs_full.astype(jnp.bfloat16)
        prob_grad = jnp.einsum(
            "qhd,khd->hqk", attended_heads, value_heads, preferred_element_type=jnp.float32
        )
        row_delta = jnp.sum(probs_full * prob_grad, axis=-1, keepdims=True)
        score_grad = (probs_full * (prob_grad - row_delta)).astype(jnp.bfloat16)
        query_grads.append(
            jnp.einsum("hqk,khd->qhd", score_grad, key_heads, preferred_element_type=jnp.float32)
            * 0.125
        )
        key_grad = (
            jnp.einsum("hqk,qhd->khd", score_grad, queries, preferred_element_type=jnp.float32)
            * 0.125
        )
        value_grad = jnp.einsum(
            "hqk,qhd->khd", probs_low, attended_heads, preferred_element_type=jnp.float32
        )
    projected_grad = jnp.concatenate(
        [
            query_grads[0].reshape(row_count, feat_width),
            key_grad.reshape(row_count, feat_width),
            value_grad.reshape(row_count, feat_width),
        ],
        axis=1,
    ).astype(jnp.bfloat16)
    w_qkv_grad = lax.dot_general(
        normed_one_low, projected_grad, (((0,), (0,)), ((), ())), preferred_element_type=jnp.float32
    )
    normed_one_grad = lax.dot_general(
        projected_grad, w_qkv, (((1,), (1,)), ((), ())), preferred_element_type=jnp.float32
    )
    tokens_part, gain1_grad = norm_one_back(normed_one_grad)
    tokens_grad = (mixed_grad + tokens_part).astype(jnp.bfloat16)
    local_counts = jnp.sum(one_hot, axis=0).astype(jnp.float32)
    gain1_sum, w_qkv_sum, w_o_sum, gain2_sum, counts = lax.psum(
        (gain1_grad, w_qkv_grad, w_o_grad, gain2_grad, local_counts), ("dp", "expert")
    )
    return (
        output.astype(jnp.bfloat16),
        tokens_grad,
        gain1_sum,
        w_qkv_sum,
        w_o_sum,
        gain2_sum,
        d_w_in,
        d_w_out,
        counts,
    )


def solution(mesh):
    placed = (
        P(("dp", "expert"), None),
        P(("dp", "expert"), None),
        P(("dp", "expert"), None),
        P(("dp", "expert"), None),
        P(("dp", "expert"), None),
        P(("dp", "expert")),
        P(),
        P(),
        P(),
        P(),
        P(),
        P(),
        P("expert", "dp", None),
        P("expert", "dp", None),
    )
    return jax.shard_map(
        body,
        mesh=mesh,
        in_specs=placed,
        out_specs=(
            P(("dp", "expert"), None),
            P(("dp", "expert"), None),
            P(),
            P(),
            P(),
            P(),
            P("expert", "dp", None),
            P("expert", "dp", None),
            P(),
        ),
        check_vma=False,
    )
```

profile of v0, /device:TPU:0, one launch (start us, length us, event | category | flops | bytes accessed | tf_op | source)
XLA Modules:
  0.0 601.5 jit_solution(12574793378495375460)
XLA Ops:
  14.4 6.2 %reduce-window.19 = s32[10,8,128]{2,1,0:T(8,128)} reduce-window(s32[10,8,128]{2,1,0:T(8,128)} %fusion.76, s32[]{:T(128)} %constant.21.clone.1), window={size=1x1x128 pad=0_0x0_0x127_0}, to_apply=%region_6.7 | reduce-window | flops 1300480 | bytes 81924 | tf_op jit(solution)/shard_map/reduce-window.1
  55.7 5.1 fusion.59
  71.9 7.2 %scatter_custom_fusion = bf16[1280,768]{1,0:T(8,128)(2,1)} fusion(s32[1024]{0:T(1024)S(1)} %bitcast.116, bf16[1024,768]{1,0:T(8,128)(2,1)} %reshape.407, bf16[]{:T(256)} %constant.25.clone.1), kind=kCustom, calls=%fused_computation.98 | custom fusion | bytes 1966592 | tf_op jit(solution)/shard_map/scatter | solution.py:115
  81.8 7.3 %all-to-all-start = ((bf16[8,128,768]{2,1,0:T(8,128)(2,1)}), bf16[8,128,768]{2,1,0:T(8,128)(2,1)}, u32[]{:S(2)}, u32[]{:S(2)}) async-start(bf16[8,128,768]{2,1,0:T(8,128)(2,1)} %bitcast.96), calls=%async_computation | async-start | bytes 3145728 | tf_op jit(solution)/shard_map/all_to_all | solution.py:119
  95.4 5.4 reshape.374
  100.8 8.1 %scatter_custom_fusion.1 = bf16[1280,768]{1,0:T(8,128)(2,1)} fusion(s32[1024]{0:T(1024)S(1)} %bitcast.117, f32[1024,768]{1,0:T(8,128)} %reshape.374, f32[1024]{0:T(1024)S(1)} %mul.298, bf16[]{:T(256)} %constant.25.clone.1), kind=kCustom, calls=%fused_computation.71 | custom fusion | flops 1572864 | bytes 5115906 | tf_op jit(solution)/shard_map/scatter | solution.py:134
  111.5 14.8 %all-to-all-done = bf16[8,128,768]{2,1,0:T(8,128)(2,1)} async-done(((bf16[8,128,768]{2,1,0:T(8,128)(2,1)}), bf16[8,128,768]{2,1,0:T(8,128)(2,1)}, u32[]{:S(2)}, u32[]{:S(2)}) %all-to-all-start) | async-done | bytes 1572896 | tf_op jit(solution)/shard_map/all_to_all | solution.py:119
  130.6 10.3 %fusion.19 = f32[1024,3072]{1,0:T(8,128)} fusion(bf16[1024,768]{1,0:T(8,128)(2,1)} %bitcast.14, bf16[1,3072,768]{2,1,0:T(8,128)(2,1)} %all-gather.3.cloned.1.call-done), kind=kOutput, calls=%fused_computation.32 | convolution fusion | flops 4831838208 | bytes 18874368 | tf_op jit(solution)/shard_map/gcd,gfd->gcf/dot_general | solution.py:19
  140.9 26.3 %all-to-all-done.2 = bf16[8,128,768]{2,1,0:T(8,128)(2,1)} async-done(((bf16[8,128,768]{2,1,0:T(8,128)(2,1)}), bf16[8,128,768]{2,1,0:T(8,128)(2,1)}, u32[]{:S(2)}, u32[]{:S(2)}) %all-to-all-start.2) | async-done | bytes 1572896 | tf_op jit(solution)/shard_map/all_to_all | solution.py:138
  167.2 11.3 %fusion.98 = f32[3072,768]{0,1:T(8,128)} fusion(bf16[1024,768]{1,0:T(8,128)(2,1)} %bitcast.22, f32[1024,3072]{1,0:T(8,128)} %fusion.19), kind=kOutput, calls=%fused_computation.147 | convolution fusion | flops 4860149760 | bytes 23592960 | tf_op jit(solution)/shard_map/dot_general | solution.py:164
  178.5 15.7 %fusion.6 = bf16[1024,3072]{1,0:T(8,128)(2,1)S(1)} fusion(f32[1024,3072]{1,0:T(8,128)} %fusion.19, bf16[1024,768]{1,0:T(8,128)(2,1)} %bitcast.22, bf16[1,3072,768]{2,1,0:T(8,128)(2,1)} %all-gather.5.cloned.1.call-done), kind=kOutput, calls=%fused_computation.13 | convolution fusion | flops 4894752768 | bytes 25165824 | tf_op jit(solution)/shard_map/gcd,gfd->gcf/dot_general | solution.py:28
  194.3 8.3 %fusion.105 = f32[3072,768]{0,1:T(8,128)S(1)} fusion(bf16[1024,3072]{1,0:T(8,128)(2,1)S(1)} %fusion.6, bf16[1024,768]{1,0:T(8,128)(2,1)} %bitcast.14), kind=kOutput, calls=%fused_computation.153 | convolution fusion | flops 4831838208 | bytes 17301504 | tf_op jit(solution)/shard_map/dot_general | solution.py:161
  202.6 6.9 %pad_maximum_fusion = f32[3072,1536]{0,1:T(8,128)} fusion(f32[3072,768]{0,1:T(8,128)S(1)} %copy-done.11, f32[3072,768]{0,1:T(8,128)S(1)} %fusion.105), kind=kLoop, calls=%fused_computation.4 | loop fusion | flops 4718592 | bytes 37748736 | tf_op jit(solution)/shard_map/concatenate | solution.py:168
  209.5 12.5 %fusion.40 = bf16[1024,768]{1,0:T(8,128)(2,1)} fusion(bf16[1,3072,768]{2,1,0:T(8,128)(2,1)} %all-gather.5.cloned.1.call-done, f32[1024,3072]{1,0:T(8,128)} %fusion.19), kind=kOutput, calls=%fused_computation.65 | convolution fusion | flops 4860936192 | bytes 18874368 | tf_op jit(solution)/shard_map/gcf,gfd->gcd/dot_general | solution.py:21
  229.5 8.9 %fusion.104 = f32[2,128,3072]{2,1,0:T(8,128)S(1)} fusion(bf16[2,128,768]{2,1,0:T(8,128)(2,1)S(1)} %bitcast.104, bf16[2,3072,768]{2,1,0:T(8,128)(2,1)} %param.24), kind=kOutput, calls=%fused_computation.152 | convolution fusion | flops 1207959552 | bytes 12976128 | tf_op jit(solution)/shard_map/gcd,gfd->gcf/dot_general | solution.py:19
  238.4 7.5 %fusion.63 = bf16[2,128,768]{2,1,0:T(8,128)(2,1)} fusion(bf16[2,3072,768]{2,1,0:T(8,128)(2,1)} %param.25, f32[2,128,3072]{2,1,0:T(8,128)S(1)} %fusion.104), kind=kOutput, calls=%fused_computation.91 | convolution fusion | flops 1215234048 | bytes 12976128 | tf_op jit(solution)/shard_map/gcf,gfd->gcd/dot_general | solution.py:21
  246.0 6.1 %fusion.37 = bf16[1024,768]{1,0:T(8,128)(2,1)} fusion(bf16[1024,3072]{1,0:T(8,128)(2,1)S(1)} %bitcast.128, bf16[1,3072,768]{2,1,0:T(8,128)(2,1)S(1)} %bitcast.123), kind=kOutput, calls=%fused_computation.64 | convolution fusion | flops 4832624640 | bytes 12582912 | tf_op jit(solution)/shard_map/gcf,gfd->gcd/dot_general | solution.py:33
  252.1 11.0 %all-to-all-done.1 = bf16[8,128,768]{2,1,0:T(8,128)(2,1)} async-done(((bf16[8,128,768]{2,1,0:T(8,128)(2,1)}), bf16[8,128,768]{2,1,0:T(8,128)(2,1)}, u32[]{:S(2)}, u32[]{:S(2)}) %all-to-all-start.1) | async-done | bytes 1572896 | tf_op jit(solution)/shard_map/all_to_all | solution.py:125
  268.9 13.3 %fusion.60 = bf16[2,128,768]{2,1,0:T(8,128)(2,1)} fusion(bf16[2,3072,768]{2,1,0:T(8,128)(2,1)} %param.24, f32[2,128,3072]{2,1,0:T(8,128)} %copy-done.19, bf16[2,128,768]{2,1,0:T(8,128)(2,1)} %bitcast.111, bf16[2,3072,768]{2,1,0:T(8,128)(2,1)} %param.25), kind=kOutput, calls=%fused_computation.90 | convolution fusion | flops 2431844352 | bytes 22806528 | tf_op jit(solution)/shard_map/gcf,gfd->gcd/dot_general | solution.py:33
  285.1 7.6 %gather_fusion = bf16[1024,768]{1,0:T(8,128)(2,1)} fusion(bf16[1280,768]{1,0:T(8,128)(2,1)} %pad_maximum_fusion.2, s32[1024]{0:T(1024)S(1)} %broadcast_clamp_fusion), kind=kCustom, calls=%fused_computation | custom fusion | bytes 3149824 | tf_op jit(solution)/shard_map/gather | solution.py:129
  292.7 11.4 %all-to-all-done.3 = bf16[8,128,768]{2,1,0:T(8,128)(2,1)} async-done(((bf16[8,128,768]{2,1,0:T(8,128)(2,1)}), bf16[8,128,768]{2,1,0:T(8,128)(2,1)}, u32[]{:S(2)}, u32[]{:S(2)}) %all-to-all-start.3) | async-done | bytes 1572896 | tf_op jit(solution)/shard_map/all_to_all | solution.py:147
  307.0 7.4 %gather_fusion.1 = bf16[1024,768]{1,0:T(8,128)(2,1)} fusion(bf16[1280,768]{1,0:T(8,128)(2,1)} %pad_maximum_fusion.3, s32[1024]{0:T(1024)S(1)} %broadcast_clamp_fusion), kind=kCustom, calls=%fused_computation.1 | custom fusion | bytes 3149824 | tf_op jit(solution)/shard_map/gather | solution.py:176
  314.4 4.9 reshape.386
  324.2 6.8 %reduce_sum.185 = f32[512,768]{1,0:T(8,128)} reduce(f32[512,2,768]{2,1,0:T(2,128)} %reshape.386, f32[]{:T(128)} %constant.18.clone.1), dimensions={1}, to_apply=%region_14.15 | reduce | flops 393216 | bytes 4718596 | tf_op jit(solution)/shard_map/reduce_sum | solution.py:175
  334.2 16.6 %multiply_reduce_fusion.1 = f32[512,768]{1,0:T(8,128)S(1)} fusion(f32[512,2,768]{2,1,0:T(2,128)S(1)} %copy-done.6, f32[512,2]{1,0:T(8,128)} %copy.66), kind=kLoop, calls=%fused_computation.46 | loop fusion | flops 1179648 | bytes 4722688 | tf_op jit(solution)/shard_map/reduce_sum | solution.py:130
  362.0 11.0 %multiply_reduce_fusion = (f32[12,512]{1,0:T(8,128)S(1)}, f32[12,512,512]{1,2,0:T(8,128)}) fusion(f32[12,512]{1,0:T(8,128)S(1)} %copy-done.25, f32[12,512,512]{1,2,0:T(8,128)} %copy-done.1, pred[512,512]{0,1:T(8,128)(4,1)S(1)} %copy-done.15, bf16[512,12,64]{0,2,1:T(8,128)(2,1)S(1)} %bitcast.100, bf16[512,12,64]{0,2,1:T(8,128)(2,1)S(1)} %bitcast.99), kind=kOutput, calls=%fused_computation.15 | convolution fusion | flops 418375680 | bytes 27049984 | tf_op jit(solution)/shard_map/qhd,khd->hqk/dot_general | solution.py:195
  374.5 7.0 %multiply_convert_fusion = bf16[12,512,512]{1,2,0:T(8,128)(2,1)S(1)} fusion(f32[12,512,512]{1,2,0:T(8,128)} %get-tuple-element.60, f32[12,512]{1,0:T(8,128)S(1)} %get-tuple-element.59, f32[12,512]{1,0:T(8,128)S(1)} %copy-done.25, f32[12,512,512]{1,2,0:T(8,128)S(1)} %bitcast.91, pred[512,512]{0,1:T(8,128)(4,1)S(1)} %copy-done.15), kind=kLoop, calls=%fused_computation.14 | loop fusion | flops 18874368 | bytes 31768576 | tf_op jit(solution)/shard_map/convert_element_type | solution.py:199
  389.9 5.3 fusion.70
  402.1 40.2 %all-reduce = (f32[768]{0:T(1024)}, f32[768]{0:T(1024)}, f32[10]{0:T(128)}) all-reduce(f32[768]{0:T(1024)} %get-tuple-element.38, f32[768]{0:T(1024)} %get-tuple-element.36, f32[10]{0:T(128)} %convert_element_type.136), channel_id=1, replica_groups=mesh['dp'=4,'expert'=8] {'dp','expert'}, use_global_device_ids=true, to_apply=%region_21.22 | all-reduce | flops 1546 | bytes 12368 | tf_op jit(solution)/shard_map/psum | solution.py:228
  446.9 5.0 slice_bitcast_fusion
  458.0 128.8 %all-reduce.4.cloned.1.call-done = (f32[768,2304]{1,0:T(8,128)}, f32[768,768]{1,0:T(8,128)}) async-done(((f32[768,2304]{1,0:T(8,128)}, f32[768,768]{1,0:T(8,128)}), (f32[768,2304]{1,0:T(8,128)}, f32[768,768]{1,0:T(8,128)})) %all-reduce.4.cloned.1.call-update) | async-done | bytes 9437200 | tf_op jit(solution)/shard_map/psum | solution.py:228
  586.8 6.6 %copy.81 = f32[768,2304]{1,0:T(8,128)} copy(f32[768,2304]{1,0:T(8,128)} %get-tuple-element.66) | data formatting | bytes 14155776
  (202 shorter events, 136.0 us)
Async XLA Ops:
  7.2 20.0 %copy-start = (bf16[768,2304]{1,0:T(8,128)(2,1)S(1)}, bf16[768,2304]{1,0:T(8,128)(2,1)}, u32[]{:S(2)}) copy-start(bf16[768,2304]{1,0:T(8,128)(2,1)} %param.21) | copy-start | bytes 10616836
  7.2 123.4 %all-gather.3.cloned.1.call-start = ((), (), s32[]{:S(2)}) async-start(), calls=%async_computation.5 | async-start | bytes 5898240 | tf_op jit(solution)/shard_map/all_gather | solution.py:70
  9.6 22.3 %copy-start.31 = (f32[512]{0:T(512)}, f32[512]{0:T(512)S(1)}, u32[]{:S(2)}) copy-start(f32[512]{0:T(512)S(1)} %broadcast_multiply_fusion.2) | copy-start | bytes 6148
  11.1 12.5 %copy-start.37 = (f32[512]{0:T(512)}, f32[512]{0:T(512)S(1)}, u32[]{:S(2)}) copy-start(f32[512]{0:T(512)S(1)} %fusion.45) | copy-start | bytes 6148
  11.1 20.7 %copy-start.35 = (f32[512]{0:T(512)}, f32[512]{0:T(512)S(1)}, u32[]{:S(2)}) copy-start(f32[512]{0:T(512)S(1)} %fusion.77) | copy-start | bytes 6148
  40.3 7.0 %copy-start.45 = (s32[512]{0:T(512)S(1)}, s32[512]{0:T(512)}, u32[]{:S(2)}) copy-start(s32[512]{0:T(512)} %param.19) | copy-start | bytes 6148
  79.1 10.7 %copy-start.44 = (f32[512,2]{0,1:T(2,128)S(1)}, f32[512,2]{0,1:T(2,128)}, u32[]{:S(2)}) copy-start(f32[512,2]{0,1:T(2,128)} %param.17) | copy-start | bytes 12292
  81.8 44.5 %all-to-all-start = ((bf16[8,128,768]{2,1,0:T(8,128)(2,1)}), bf16[8,128,768]{2,1,0:T(8,128)(2,1)}, u32[]{:S(2)}, u32[]{:S(2)}) async-start(bf16[8,128,768]{2,1,0:T(8,128)(2,1)} %bitcast.96), calls=%async_computation | async-start | bytes 3145728 | tf_op jit(solution)/shard_map/all_to_all | solution.py:119
  89.1 89.4 %all-gather.5.cloned.1.call-start = ((), (), s32[]{:S(2)}) async-start(), calls=%async_computation.6 | async-start | bytes 5898240 | tf_op jit(solution)/shard_map/all_gather | solution.py:71
  126.2 40.9 %all-to-all-start.2 = ((bf16[8,128,768]{2,1,0:T(8,128)(2,1)}), bf16[8,128,768]{2,1,0:T(8,128)(2,1)}, u32[]{:S(2)}, u32[]{:S(2)}) async-start(bf16[8,128,768]{2,1,0:T(8,128)(2,1)} %bitcast.97), calls=%async_computation.2 | async-start | bytes 3145728 | tf_op jit(solution)/shard_map/all_to_all | solution.py:138
  130.5 316.4 %reduce-scatter.2.cloned.1.call-start = ((), (), s32[]{:S(2)}) async-start(), calls=%async_computation.7 | async-start | bytes 23592960 | tf_op jit(solution)/shard_map/reduce_scatter | solution.py:167
  194.3 8.3 %copy-start.49 = (bf16[1024,3072]{1,0:T(8,128)(2,1)}, bf16[1024,3072]{1,0:T(8,128)(2,1)S(1)}, u32[]{:S(2)}) copy-start(bf16[1024,3072]{1,0:T(8,128)(2,1)S(1)} %fusion.6) | copy-start | bytes 18874372
  194.3 8.3 %copy-start.11 = (f32[3072,768]{0,1:T(8,128)S(1)}, f32[3072,768]{0,1:T(8,128)}, u32[]{:S(2)}) copy-start(f32[3072,768]{0,1:T(8,128)} %fusion.98) | copy-start | bytes 28311556
  222.0 41.1 %all-to-all-start.1 = ((bf16[8,128,768]{2,1,0:T(8,128)(2,1)}), bf16[8,128,768]{2,1,0:T(8,128)(2,1)}, u32[]{:S(2)}, u32[]{:S(2)}) async-start(bf16[8,128,768]{2,1,0:T(8,128)(2,1)} %bitcast.106), calls=%async_computation.1 | async-start | bytes 3145728 | tf_op jit(solution)/shard_map/all_to_all | solution.py:125
  229.5 16.4 %slice-start.3 = ((s8[4718592]{0:T(1024)(128)(4,1)}), s8[524288]{0:T(1024)(128)(4,1)S(1)}, s32[]{:S(2)}) async-start(s8[4718592]{0:T(1024)(128)(4,1)} %bitcast.122), calls=%async_computation.12 | async-start | bytes 1048576
  229.5 16.4 %slice-start.5 = ((s8[6291456]{0:T(1024)(128)(4,1)}), s8[4194304]{0:T(1024)(128)(4,1)S(1)}, s32[]{:S(2)}) async-start(s8[6291456]{0:T(1024)(128)(4,1)} %bitcast.127), calls=%async_computation.14 | async-start | bytes 8388608
  238.4 7.5 %copy-start.19 = (f32[2,128,3072]{2,1,0:T(8,128)}, f32[2,128,3072]{2,1,0:T(8,128)S(1)}, u32[]{:S(2)}) copy-start(f32[2,128,3072]{2,1,0:T(8,128)S(1)} %fusion.104) | copy-start | bytes 9437188
  238.4 7.5 %slice-start.4 = ((s8[4718592]{0:T(1024)(128)(4,1)}), s8[4194304]{0:T(1024)(128)(4,1)S(1)}, s32[]{:S(2)}) async-start(s8[4718592]{0:T(1024)(128)(4,1)} %bitcast.122), calls=%async_computation.13 | async-start | bytes 8388608
  238.4 7.5 %slice-start.6 = ((s8[6291456]{0:T(1024)(128)(4,1)}), s8[2097152]{0:T(1024)(128)(4,1)S(1)}, s32[]{:S(2)}) async-start(s8[6291456]{0:T(1024)(128)(4,1)} %bitcast.127), calls=%async_computation.15 | async-start | bytes 4194304
  263.1 40.9 %all-to-all-start.3 = ((bf16[8,128,768]{2,1,0:T(8,128)(2,1)}), bf16[8,128,768]{2,1,0:T(8,128)(2,1)}, u32[]{:S(2)}, u32[]{:S(2)}) async-start(bf16[8,128,768]{2,1,0:T(8,128)(2,1)} %bitcast.105), calls=%async_computation.3 | async-start | bytes 3145728 | tf_op jit(solution)/shard_map/all_to_all | solution.py:147
  267.5 319.3 %all-reduce.4.cloned.1.call-start = ((), (), s32[]{:S(2)}) async-start(), calls=%async_computation.8 | async-start | bytes 18874368 | tf_op jit(solution)/shard_map/psum | solution.py:228
  324.1 6.8 %copy-start.28 = (f32[512]{0:T(512)S(1)}, f32[512]{0:T(512)}, u32[]{:S(2)}) copy-start(f32[512]{0:T(512)} %copy-done.27) | copy-start | bytes 6148
  324.1 6.8 %copy-start.30 = (f32[768]{0:T(1024)S(1)}, f32[768]{0:T(1024)}, u32[]{:S(2)}) copy-start(f32[768]{0:T(1024)} %param.23) | copy-start | bytes 9220
  324.1 6.8 %copy-start.34 = (f32[512]{0:T(512)S(1)}, f32[512]{0:T(512)}, u32[]{:S(2)}) copy-start(f32[512]{0:T(512)} %copy-done.33) | copy-start | bytes 6148
  324.1 10.0 %copy-start.40 = (f32[512]{0:T(512)S(1)}, f32[512]{0:T(512)}, u32[]{:S(2)}) copy-start(f32[512]{0:T(512)} %copy-done.39) | copy-start | bytes 6148
  334.1 16.7 %copy-start.3 = (f32[512,768]{1,0:T(8,128)S(1)}, f32[512,768]{1,0:T(8,128)}, u32[]{:S(2)}) copy-start(f32[512,768]{1,0:T(8,128)} %copy-done.2) | copy-start | bytes 4718596
  334.2 16.7 %copy-start.4 = (f32[512,768]{1,0:T(8,128)S(1)}, f32[512,768]{1,0:T(8,128)}, u32[]{:S(2)}) copy-start(f32[512,768]{1,0:T(8,128)} %reduce_sum.185) | copy-start | bytes 4718596
  361.9 11.1 %slice-start = ((s8[12582912]{0:T(1024)(128)(4,1)}), s8[4194304]{0:T(1024)(128)(4,1)S(1)}, s32[]{:S(2)}) async-start(s8[12582912]{0:T(1024)(128)(4,1)} %bitcast.90), calls=%async_computation.9 | async-start | bytes 8388608
  361.9 11.1 %slice-start.1 = ((s8[12582912]{0:T(1024)(128)(4,1)}), s8[4194304]{0:T(1024)(128)(4,1)S(1)}, s32[]{:S(2)}) async-start(s8[12582912]{0:T(1024)(128)(4,1)} %bitcast.90), calls=%async_computation.10 | async-start | bytes 8388608
  361.9 12.6 %slice-start.2 = ((s8[12582912]{0:T(1024)(128)(4,1)}), s8[4194304]{0:T(1024)(128)(4,1)S(1)}, s32[]{:S(2)}) async-start(s8[12582912]{0:T(1024)(128)(4,1)} %bitcast.90), calls=%async_computation.11 | async-start | bytes 8388608
  374.5 7.1 %copy-start.12 = (bf16[512,768]{0,1:T(8,128)(2,1)S(1)}, bf16[512,768]{0,1:T(8,128)(2,1)}, u32[]{:S(2)}) copy-start(bf16[512,768]{0,1:T(8,128)(2,1)} %copy.58) | copy-start | bytes 2359300
  586.8 6.6 %copy-start.21 = (f32[768,768]{1,0:T(8,128)S(1)}, f32[768,768]{1,0:T(8,128)}, u32[]{:S(2)}) copy-start(f32[768,768]{1,0:T(8,128)} %get-tuple-element.67) | copy-start | bytes 7077892
  (33 other events, 110.8 us)
Sparse Core Ops, SparseCore 0:
  9.6 40.1 all-gather.2
  91.5 38.8 all-gather.4
  209.6 138.4 reduce-scatter.1
  395.4 191.3 all-reduce.3
where the time goes:
time: 612 us; the launch traced here: 601 us
  waiting for transfers between devices  194 us (32%)
  matrix products  142 us (23%)
  local copies, waits for them, and re-layouts  107 us (17%)
  other arithmetic  83.7 us (14%)
  blocking collectives  40.2 us (7%)
  starting transfers between devices  20.6 us (3%)
  between operations  14.7 us (2%)
    psum x1, waiting for transfers between devices, body(): lax.psum((gain1_grad, w_qkv_grad, w_o_grad, gain2_grad, local_counts), ('...  129 us
    psum x1, blocking collectives, body(): lax.psum((gain1_grad, w_qkv_grad, w_o_grad, gain2_grad, local_counts), ('...  40.2 us
    all_to_all x1, waiting for transfers between devices, body(): lax.all_to_all(routed_grad, 'expert', split_axis=0, concat_axis=0, tiled=...  26.3 us
    unnamed x122, local copies, waits for them, and re-layouts  23.9 us
    dot_general x2, matrix products, expert_forward(): jnp.einsum('gcf,gfd->gcd', active, down_weights, preferred_element_type=j...  20 us
    dot_general x2, matrix products, expert_backward(): jnp.einsum('gcf,gfd->gcd', hidden_grad, up_weights, preferred_element_typ...  19.5 us
    dot_general x2, matrix products, expert_forward(): jnp.einsum('gcd,gfd->gcf', rows_low, up_weights, preferred_element_type=j...  19.2 us
    reduce_sum x1, other arithmetic, body(): output = mixed_rows + jnp.sum(picked * gates[:, :, None], axis=1)  16.6 us
  transfers between devices with their start and end apart: 8, of which 5 were waited for; matrix products, arithmetic and copies ran while one was open for 48% of the time, Pallas kernels for 0%

commit v1 on v0

--- a/solution.py
+++ b/solution.py
@@ -226,7 +226,7 @@
     tokens_grad = (mixed_grad + tokens_part).astype(jnp.bfloat16)
     local_counts = jnp.sum(one_hot, axis=0).astype(jnp.float32)
     gain1_sum, w_qkv_sum, w_o_sum, gain2_sum, counts = lax.psum(
-        (gain1_grad, w_qkv_grad, w_o_grad, gain2_grad, local_counts), ("dp", "expert")
+        lax.psum((gain1_grad, w_qkv_grad, w_o_grad, gain2_grad, local_counts), "expert"), "dp"
     )
     return (
         output.astype(jnp.bfloat16),

time: 612 us -> 981 us (1.60)
  waiting for transfers between devices: 194 us -> 574 us
  blocking collectives: 40.2 us -> 27.1 us
    psum x1 -> x2, waiting for transfers between devices: 129 us -> 435 us  [the longest x1 274 us: body(): lax.psum((gain1_grad, w_qkv_grad, w_o_grad, gain2_grad, local_counts), 'e...]
    reduce_scatter x1, waiting for transfers between devices: 0.01 us -> 102 us  [body(): lax.psum_scatter(jnp.concatenate([term_in, term_out], axis=1), 'dp', scat...]
    all_to_all x1, waiting for transfers between devices: 14.8 us -> 0.01 us  [body(): lax.all_to_all(routed_rows, 'expert', split_axis=0, concat_axis=0, tiled=...]
    psum x1 -> x2, blocking collectives: 40.2 us -> 27.1 us  [the longest x1 20.5 us: body(): lax.psum((gain1_grad, w_qkv_grad, w_o_grad, gain2_grad, local_counts), 'e...]
    all_to_all x1, waiting for transfers between devices: 26.3 us -> 13.6 us  [body(): lax.all_to_all(routed_grad, 'expert', split_axis=0, concat_axis=0, tiled=...]
    unnamed x122 -> x104, local copies, waits for them, and re-layouts: 23.9 us -> 25 us
  transfers between devices with their start and end apart: 8 -> 9, of which waited for: 5 -> 6; matrix products, arithmetic and copies ran while one was open for 48% -> 23% of each run, Pallas kernels for 0% -> 0%
where the time goes in v1:
time: 981 us; the launch traced here: 969 us
  waiting for transfers between devices  574 us (59%)
  matrix products  137 us (14%)
  local copies, waits for them, and re-layouts  107 us (11%)
  other arithmetic  87.5 us (9%)
  blocking collectives  27.1 us (3%)
  starting transfers between devices  22.8 us (2%)
  between operations  14.6 us (1%)
    psum x1, waiting for transfers between devices, body(): lax.psum((gain1_grad, w_qkv_grad, w_o_grad, gain2_grad, local_counts), 'e...  274 us
    psum x1, waiting for transfers between devices, body(): lax.psum(lax.psum((gain1_grad, w_qkv_grad, w_o_grad, gain2_grad, local_co...  162 us
    reduce_scatter x1, waiting for transfers between devices, body(): lax.psum_scatter(jnp.concatenate([term_in, term_out], axis=1), 'dp', scat...  102 us
    unnamed x104, local copies, waits for them, and re-layouts  25 us
    dot_general x2, matrix products, expert_backward(): jnp.einsum('gcf,gfd->gcd', hidden_grad, up_weights, preferred_element_typ...  21.5 us
    psum x1, blocking collectives, body(): lax.psum((gain1_grad, w_qkv_grad, w_o_grad, gain2_grad, local_counts), 'e...  20.5 us
  transfers between devices with their start and end apart: 9, of which 6 were waited for; matrix products, arithmetic and copies ran while one was open for 23% of the time, Pallas kernels for 0%

profile of v1, /device:TPU:0, one launch (start us, length us, event | category | flops | bytes accessed | tf_op | source)
XLA Modules:
  0.0 968.9 jit_solution(10841037743876898147)
XLA Ops:
  22.5 6.2 reduce-window.19
  71.6 7.3 scatter_custom_fusion
  81.5 7.5 all-to-all-start
  100.6 8.0 scatter_custom_fusion.1
  113.1 6.8 fusion.104
  121.5 6.3 fusion.63
  127.8 6.0 all-to-all-start.2
  133.8 10.3 %fusion.19 = f32[1024,3072]{1,0:T(8,128)} fusion(bf16[1024,768]{1,0:T(8,128)(2,1)} %bitcast.14, bf16[1,3072,768]{2,1,0:T(8,128)(2,1)} %all-gather.3.cloned.1.call-done), kind=kOutput, calls=%fused_computation.32 | convolution fusion | flops 4831838208 | bytes 18874368 | tf_op jit(solution)/shard_map/gcd,gfd->gcf/dot_general | solution.py:19
  144.1 12.5 %fusion.40 = bf16[1024,768]{1,0:T(8,128)(2,1)} fusion(bf16[1,3072,768]{2,1,0:T(8,128)(2,1)} %all-gather.5.cloned.1.call-done, f32[1024,3072]{1,0:T(8,128)} %fusion.19), kind=kOutput, calls=%fused_computation.65 | convolution fusion | flops 4860936192 | bytes 18874368 | tf_op jit(solution)/shard_map/gcf,gfd->gcd/dot_general | solution.py:21
  156.6 13.6 %all-to-all-done.2 = bf16[8,128,768]{2,1,0:T(8,128)(2,1)} async-done(((bf16[8,128,768]{2,1,0:T(8,128)(2,1)}), bf16[8,128,768]{2,1,0:T(8,128)(2,1)}, u32[]{:S(2)}, u32[]{:S(2)}) %all-to-all-start.2) | async-done | bytes 1572896 | tf_op jit(solution)/shard_map/all_to_all | solution.py:138
  175.0 15.3 %fusion.6 = bf16[1024,3072]{1,0:T(8,128)(2,1)S(1)} fusion(f32[1024,3072]{1,0:T(8,128)} %fusion.19, bf16[1024,768]{1,0:T(8,128)(2,1)} %bitcast.22, bf16[1,3072,768]{2,1,0:T(8,128)(2,1)} %all-gather.5.cloned.1.call-done), kind=kOutput, calls=%fused_computation.13 | convolution fusion | flops 4894752768 | bytes 25165824 | tf_op jit(solution)/shard_map/gcd,gfd->gcf/dot_general | solution.py:28
  192.9 8.5 fusion.37
  201.4 10.2 %all-to-all-done.1 = bf16[8,128,768]{2,1,0:T(8,128)(2,1)} async-done(((bf16[8,128,768]{2,1,0:T(8,128)(2,1)}), bf16[8,128,768]{2,1,0:T(8,128)(2,1)}, u32[]{:S(2)}, u32[]{:S(2)}) %all-to-all-start.1) | async-done | bytes 1572896 | tf_op jit(solution)/shard_map/all_to_all | solution.py:125
  218.0 13.0 %fusion.60 = bf16[2,128,768]{2,1,0:T(8,128)(2,1)} fusion(bf16[2,3072,768]{2,1,0:T(8,128)(2,1)} %param.24, f32[2,128,3072]{2,1,0:T(8,128)} %copy-done.17, bf16[2,128,768]{2,1,0:T(8,128)(2,1)} %bitcast.111, bf16[2,3072,768]{2,1,0:T(8,128)(2,1)} %param.25), kind=kOutput, calls=%fused_computation.90 | convolution fusion | flops 2431844352 | bytes 22806528 | tf_op jit(solution)/shard_map/gcf,gfd->gcd/dot_general | solution.py:33
  233.9 7.5 gather_fusion
  241.4 11.1 %all-to-all-done.3 = bf16[8,128,768]{2,1,0:T(8,128)(2,1)} async-done(((bf16[8,128,768]{2,1,0:T(8,128)(2,1)}), bf16[8,128,768]{2,1,0:T(8,128)(2,1)}, u32[]{:S(2)}, u32[]{:S(2)}) %all-to-all-start.3) | async-done | bytes 1572896 | tf_op jit(solution)/shard_map/all_to_all | solution.py:147
  255.4 7.4 gather_fusion.1
  267.6 6.8 reduce_sum.185
  282.9 16.6 %multiply_reduce_fusion.1 = f32[512,768]{1,0:T(8,128)S(1)} fusion(f32[512,2,768]{2,1,0:T(2,128)} %reshape.385, f32[512,2]{1,0:T(8,128)} %copy.66), kind=kLoop, calls=%fused_computation.46 | loop fusion | flops 1179648 | bytes 4722688 | tf_op jit(solution)/shard_map/reduce_sum | solution.py:130
  307.6 8.1 fusion.56
  315.7 9.8 %multiply_reduce_fusion = (f32[12,512]{1,0:T(8,128)S(1)}, f32[12,512,512]{1,2,0:T(8,128)}) fusion(f32[12,512]{1,0:T(8,128)S(1)} %copy-done.24, f32[12,512,512]{1,2,0:T(8,128)} %copy-done.1, pred[512,512]{0,1:T(8,128)(4,1)S(1)} %copy-done.13, bf16[512,12,64]{0,2,1:T(8,128)(2,1)S(1)} %bitcast.102, bf16[512,12,64]{0,2,1:T(8,128)(2,1)S(1)} %bitcast.100), kind=kOutput, calls=%fused_computation.15 | convolution fusion | flops 418375680 | bytes 27049984 | tf_op jit(solution)/shard_map/qhd,khd->hqk/dot_general | solution.py:195
  325.5 7.4 multiply_convert_fusion
  337.1 5.3 fusion.70
  342.4 7.7 fusion.105
  350.1 9.1 fusion.98
  359.3 7.3 pad_maximum_fusion
  366.8 273.7 %all-reduce.7.cloned.1.call-done = (f32[768,2304]{1,0:T(8,128)}, f32[768,768]{1,0:T(8,128)}) async-done(((f32[768,2304]{1,0:T(8,128)}, f32[768,768]{1,0:T(8,128)}), (f32[768,2304]{1,0:T(8,128)}, f32[768,768]{1,0:T(8,128)})) %all-reduce.7.cloned.1.call-update) | async-done | bytes 9437200 | tf_op jit(solution)/shard_map/psum | solution.py:229
  647.3 20.5 %all-reduce = (f32[768]{0:T(1024)}, f32[768]{0:T(1024)}, f32[10]{0:T(128)}) all-reduce(f32[768]{0:T(1024)} %get-tuple-element.38, f32[768]{0:T(1024)} %get-tuple-element.36, f32[10]{0:T(128)} %convert_element_type.136), channel_id=1, replica_groups=mesh['dp'=4,'expert'=8] {'expert'}, use_global_device_ids=true, to_apply=%region_21.22 | all-reduce | flops 1546 | bytes 12368 | tf_op jit(solution)/shard_map/psum | solution.py:229
  667.8 6.6 all-reduce.2
  679.5 101.9 %reduce-scatter.2.cloned.1.call-done = f32[768,1536]{0,1:T(8,128)} async-done(((f32[3072,1536]{0,1:T(8,128)}), f32[768,1536]{0,1:T(8,128)}) %reduce-scatter.2.cloned.1.call-update) | async-done | bytes 4718608 | tf_op jit(solution)/shard_map/reduce_scatter | solution.py:167
  792.6 161.6 %all-reduce.9.cloned.1.call-done = (f32[768,2304]{1,0:T(8,128)}, f32[768,768]{1,0:T(8,128)}) async-done(((f32[768,2304]{1,0:T(8,128)}, f32[768,768]{1,0:T(8,128)}), (f32[768,2304]{1,0:T(8,128)}, f32[768,768]{1,0:T(8,128)})) %all-reduce.9.cloned.1.call-update) | async-done | bytes 9437200 | tf_op jit(solution)/shard_map/psum | solution.py:228
  954.2 6.6 copy.83
  (187 shorter events, 148.1 us)
Async XLA Ops:
  7.2 28.1 %copy-start = (bf16[768,2304]{1,0:T(8,128)(2,1)S(1)}, bf16[768,2304]{1,0:T(8,128)(2,1)}, u32[]{:S(2)}) copy-start(bf16[768,2304]{1,0:T(8,128)(2,1)} %param.21) | copy-start | bytes 10616836
  7.2 7.2 copy-start.39
  7.2 7.7 copy-start.42
  7.2 126.6 %all-gather.3.cloned.1.call-start = ((), (), s32[]{:S(2)}) async-start(), calls=%async_computation.5 | async-start | bytes 5898240 | tf_op jit(solution)/shard_map/all_gather | solution.py:70
  7.9 136.2 %all-gather.5.cloned.1.call-start = ((), (), s32[]{:S(2)}) async-start(), calls=%async_computation.6 | async-start | bytes 5898240 | tf_op jit(solution)/shard_map/all_gather | solution.py:71
  16.4 22.1 %copy-start.27 = (f32[512]{0:T(512)}, f32[512]{0:T(512)S(1)}, u32[]{:S(2)}) copy-start(f32[512]{0:T(512)S(1)} %broadcast_multiply_fusion.2) | copy-start | bytes 6148
  18.0 13.7 %copy-start.30 = (f32[512]{0:T(512)}, f32[512]{0:T(512)S(1)}, u32[]{:S(2)}) copy-start(f32[512]{0:T(512)S(1)} %fusion.45) | copy-start | bytes 6148
  40.0 7.0 copy-start.38
  54.5 5.7 copy-start.25
  61.5 7.9 copy-start.32
  71.6 9.9 %copy-start.34 = (s32[1024,1]{0,1:T(1,128)}, s32[1024,1]{0,1:T(1,128)S(1)}, u32[]{:S(2)}) copy-start(s32[1024,1]{0,1:T(1,128)S(1)} %compare_select_fusion) | copy-start | bytes 12292
  81.5 46.3 %all-to-all-start = ((bf16[8,128,768]{2,1,0:T(8,128)(2,1)}), bf16[8,128,768]{2,1,0:T(8,128)(2,1)}, u32[]{:S(2)}, u32[]{:S(2)}) async-start(bf16[8,128,768]{2,1,0:T(8,128)(2,1)} %bitcast.98), calls=%async_computation | async-start | bytes 3145728 | tf_op jit(solution)/shard_map/all_to_all | solution.py:119
  127.8 42.4 %all-to-all-start.2 = ((bf16[8,128,768]{2,1,0:T(8,128)(2,1)}), bf16[8,128,768]{2,1,0:T(8,128)(2,1)}, u32[]{:S(2)}, u32[]{:S(2)}) async-start(bf16[8,128,768]{2,1,0:T(8,128)(2,1)} %bitcast.97), calls=%async_computation.2 | async-start | bytes 3145728 | tf_op jit(solution)/shard_map/all_to_all | solution.py:138
  170.3 41.3 %all-to-all-start.1 = ((bf16[8,128,768]{2,1,0:T(8,128)(2,1)}), bf16[8,128,768]{2,1,0:T(8,128)(2,1)}, u32[]{:S(2)}, u32[]{:S(2)}) async-start(bf16[8,128,768]{2,1,0:T(8,128)(2,1)} %bitcast.106), calls=%async_computation.1 | async-start | bytes 3145728 | tf_op jit(solution)/shard_map/all_to_all | solution.py:125
  211.6 40.9 %all-to-all-start.3 = ((bf16[8,128,768]{2,1,0:T(8,128)(2,1)}), bf16[8,128,768]{2,1,0:T(8,128)(2,1)}, u32[]{:S(2)}, u32[]{:S(2)}) async-start(bf16[8,128,768]{2,1,0:T(8,128)(2,1)} %bitcast.105), calls=%async_computation.3 | async-start | bytes 3145728 | tf_op jit(solution)/shard_map/all_to_all | solution.py:147
  215.9 424.5 %all-reduce.7.cloned.1.call-start = ((), (), s32[]{:S(2)}) async-start(), calls=%async_computation.8 | async-start | bytes 18874368 | tf_op jit(solution)/shard_map/psum | solution.py:229
  267.6 9.8 %copy-start.33 = (f32[512]{0:T(512)S(1)}, f32[512]{0:T(512)}, u32[]{:S(2)}) copy-start(f32[512]{0:T(512)} %copy-done.32) | copy-start | bytes 6148
  282.9 16.6 %copy-start.3 = (f32[512,768]{1,0:T(8,128)S(1)}, f32[512,768]{1,0:T(8,128)}, u32[]{:S(2)}) copy-start(f32[512,768]{1,0:T(8,128)} %copy-done.2) | copy-start | bytes 4718596
  282.9 16.6 %copy-start.4 = (f32[512,768]{1,0:T(8,128)S(1)}, f32[512,768]{1,0:T(8,128)}, u32[]{:S(2)}) copy-start(f32[512,768]{1,0:T(8,128)} %reduce_sum.185) | copy-start | bytes 4718596
  282.9 16.7 %copy-start.37 = (f32[512]{0:T(512)S(1)}, f32[512]{0:T(512)}, u32[]{:S(2)}) copy-start(f32[512]{0:T(512)} %multiply_multiply_fusion.5) | copy-start | bytes 6148
  307.6 8.1 copy-start.13
  307.6 8.1 copy-start.15
  307.6 8.1 copy-start.16
  307.6 8.1 copy-start.24
  307.6 17.9 %slice-start = ((s8[12582912]{0:T(1024)(128)(4,1)}), s8[4194304]{0:T(1024)(128)(4,1)S(1)}, s32[]{:S(2)}) async-start(s8[12582912]{0:T(1024)(128)(4,1)} %bitcast.90), calls=%async_computation.10 | async-start | bytes 8388608
  307.6 17.9 %slice-start.1 = ((s8[12582912]{0:T(1024)(128)(4,1)}), s8[4194304]{0:T(1024)(128)(4,1)S(1)}, s32[]{:S(2)}) async-start(s8[12582912]{0:T(1024)(128)(4,1)} %bitcast.90), calls=%async_computation.11 | async-start | bytes 8388608
  315.7 20.5 %copy-start.43 = (bf16[12,64,512]{2,1,0:T(8,128)(2,1)}, bf16[12,64,512]{2,1,0:T(8,128)(2,1)S(1)}, u32[]{:S(2)}) copy-start(bf16[12,64,512]{2,1,0:T(8,128)(2,1)S(1)} %fusion.56) | copy-start | bytes 2359300
  315.7 9.8 %slice-start.2 = ((s8[12582912]{0:T(1024)(128)(4,1)}), s8[4194304]{0:T(1024)(128)(4,1)S(1)}, s32[]{:S(2)}) async-start(s8[12582912]{0:T(1024)(128)(4,1)} %bitcast.90), calls=%async_computation.12 | async-start | bytes 8388608
  325.5 7.4 copy-start.10
  342.4 439.0 %reduce-scatter.2.cloned.1.call-start = ((), (), s32[]{:S(2)}) async-start(), calls=%async_computation.7 | async-start | bytes 23592960 | tf_op jit(solution)/shard_map/reduce_scatter | solution.py:167
  366.5 587.7 %all-reduce.9.cloned.1.call-start = ((), (), s32[]{:S(2)}) async-start(), calls=%async_computation.9 | async-start | bytes 18874368 | tf_op jit(solution)/shard_map/psum | solution.py:228
  954.2 6.6 copy-start.19
  (26 other events, 69.1 us)
Sparse Core Ops, SparseCore 0:
  9.6 40.1 all-gather.2
  51.4 37.4 all-gather.4
  342.5 297.8 all-reduce.6
  642.9 138.4 reduce-scatter.1
  784.0 170.1 all-reduce.8
